TPU v7x, 512 devices: a whole 4x4x16 slice. The times are simulated.
512 devices in a mesh: dp: 16 (over z_hi, y), expert: 32 (over z_lo, x, core).
Axes of the slice: x: 4, y: 4, z: 16 (z_hi: 4, z_lo: 4; z = z_hi * 4 + z_lo), core: 2. Of those that a mesh axis runs over, the one named last changes fastest.
Arguments:
- tokens: bfloat16 [57344, 1024], P(('dp', 'expert')), parts along dimension 0, may hold values from -6 to 6
- expert_ids: int32 [57344, 8], P(('dp', 'expert')), parts along dimension 0, may hold values from 0 to 31, all different within a row; in each aligned block of 112 rows (0 to 111, 112 to 223, ...) at most 56 rows name the same one
- gate_probs: float32 [57344, 8], P(('dp', 'expert')), parts along dimension 0, may hold values from 0.05 to 0.5
- w_gate: bfloat16 [32, 1024, 384], P('expert'), may hold values from -0.1875 to 0.1875
- w_up: bfloat16 [32, 1024, 384], P('expert'), may hold values from -0.1875 to 0.1875
- w_down: bfloat16 [32, 384, 1024], P('expert'), may hold values from -0.3125 to 0.3125
- placement: int32 [32], replicated, may hold values from 0 to 31, each once
- swap_flags: int32 [32], replicated, may hold values from 0 to 1, as said below
Outputs:
- mixed: bfloat16 [57344, 1024], P(('dp', 'expert')), parts along dimension 0
- stored_gate: bfloat16 [512, 1024, 384], P(('dp', 'expert')), parts along dimension 0
- stored_up: bfloat16 [512, 1024, 384], P(('dp', 'expert')), parts along dimension 0
- stored_down: bfloat16 [512, 384, 1024], P(('dp', 'expert')), parts along dimension 0
There are 16 independent parts, one for each index of `dp`. A program takes and returns all parts, laid end to end along the dimension named above; an argument that names none is the same for every part. Nothing has to cross between parts.
Inputs may be any that keep to these rules, and one draw needn't show every extreme that they name: `expert_ids`: each row names 8 different experts; the 112 rows of one device name one expert at most 56 times, a bound that some block reaches. `placement`: each expert is stored on exactly one device. swap_flags[d] equals swap_flags[d XOR (16)]; the number of devices is a power of two. The first and last pairs always trade, the second pair never does.
All inputs are finite; a program needn't handle non-finite values.
Results may differ from a plain program's by a relative error of at most 0.0057.
Values may be sent and summed in bfloat16 or wider, within the bound.
A program may use at most 64 MiB of HBM per device.

v0:
```python
import jax
import jax.numpy as jnp
from jax import lax
from jax.sharding import PartitionSpec as P


def swapped(value, axis, distance):
    mask = 2**distance
    pairs = [(source, source ^ mask) for source in range(lax.axis_size(axis))]
    return lax.ppermute(value, axis, pairs)


def expert_apply(rows, gate_w, up_w, down_w):
    gate = jnp.dot(rows, gate_w, preferred_element_type=jnp.float32)
    upward = jnp.dot(rows, up_w, preferred_element_type=jnp.float32)
    hidden = (jax.nn.silu(gate) * upward).astype(jnp.bfloat16)
    return jnp.dot(hidden, down_w, preferred_element_type=jnp.float32).astype(jnp.bfloat16)


def per_device(tokens, expert_ids, gate_probs, w_gate, w_up, w_down, placement, swap_flags):
    count_dev = lax.axis_size("expert")
    own_index = lax.axis_index("expert")
    half_axis = count_dev // 2
    partner_bit = count_dev.bit_length() - 2
    tok_rows = tokens.shape[0]
    width = tokens.shape[1]
    top_count = expert_ids.shape[1]
    capacity = min(tok_rows, 2 * tok_rows * top_count // count_dev)
    devices = jnp.arange(count_dev, dtype=jnp.int32)
    partners = jnp.bitwise_xor(devices, half_axis)
    taken = swap_flags[own_index] == 1
    moved = swapped((w_gate, w_up, w_down), "expert", partner_bit)
    stored_gate = jnp.where(taken, moved[0], w_gate)
    stored_up = jnp.where(taken, moved[1], w_up)
    stored_down = jnp.where(taken, moved[2], w_down)
    gate_w = stored_gate[0]
    up_w = stored_up[0]
    down_w = stored_down[0]
    served_by = jnp.where(swap_flags == 1, placement[partners], placement)
    matches = served_by[None, :] == devices[:, None]
    owner = jnp.sum(jnp.where(matches, devices[None, :], 0), axis=1)
    flat_ids = expert_ids.reshape(-1)
    onehot = (flat_ids[:, None] == devices[None, :]).astype(jnp.int32)
    target = jnp.sum(onehot * owner[None, :], axis=1)
    slot_index = jnp.sum(onehot * (jnp.cumsum(onehot, axis=0) - 1), axis=1)
    token_of = jnp.arange(flat_ids.shape[0], dtype=jnp.int32) // top_count
    table = (
        jnp.full((count_dev, capacity), tok_rows, jnp.int32).at[target, slot_index].set(token_of)
    )
    padded = jnp.concatenate([tokens, jnp.zeros((1, width), tokens.dtype)], axis=0)
    outgoing = padded[table]
    received = lax.all_to_all(outgoing, "expert", split_axis=0, concat_axis=0, tiled=True)
    shaped = received.shape
    computed = expert_apply(received.reshape(-1, width), gate_w, up_w, down_w).reshape(shaped)
    returned = lax.all_to_all(computed, "expert", split_axis=0, concat_axis=0, tiled=True)
    picked_rows = returned.reshape(-1, width)[target * capacity + slot_index]
    weighted = (
        picked_rows.astype(jnp.float32).reshape(tok_rows, top_count, width) * gate_probs[:, :, None]
    )
    mixed = jnp.sum(weighted, axis=1)
    return (mixed.astype(jnp.bfloat16), stored_gate, stored_up, stored_down)


def solution(mesh):
    in_specs = (
        P(("dp", "expert"), None),
        P(("dp", "expert"), None),
        P(("dp", "expert"), None),
        P("expert", None, None),
        P("expert", None, None),
        P("expert", None, None),
        P(),
        P(),
    )
    out_specs = (
        P(("dp", "expert"), None),
        P(("dp", "expert"), None, None),
        P(("dp", "expert"), None, None),
        P(("dp", "expert"), None, None),
    )
    return jax.shard_map(
        per_device, mesh=mesh, in_specs=in_specs, out_specs=out_specs, check_vma=False
    )
```

profile of v0, /device:TPU:1, one launch (start us, length us, event | category | flops | bytes accessed | tf_op | source)
XLA Modules:
  0.0 367.6 jit_solution(12917191304533828806)
XLA Ops:
  0.6 0.8 copy.17
  1.6 2.0 reduce-window.6
  3.7 0.3 slice_reduce_fusion
  4.0 1.4 gather_fusion
  5.4 0.7 compare_select_fusion.5
  6.4 45.7 %scatter_fusion = s32[32,56]{1,0:T(8,128)S(1)} fusion(s32[32,56]{1,0:T(8,128)S(1)} %broadcast_in_dim.16, s32[896]{0:T(1024)S(1)} %get-tuple-element.5, s32[896]{0:T(1024)S(1)} %add_select_fusion), kind=kCustom, calls=%fused_computation.3 | custom fusion | bytes 17920 | tf_op jit(solution)/shard_map/scatter | solution.py:48
  52.2 6.6 %gather_fusion.1 = bf16[1792,1024]{1,0:T(8,128)(2,1)} fusion(bf16[113,1024]{1,0:T(8,128)(2,1)S(1)} %concatenate.6, s32[2048]{0:T(1024)S(1)} %pad_clamp_fusion), kind=kCustom, calls=%fused_computation.1 | custom fusion | bytes 7347200 | tf_op jit(solution)/shard_map/gather | solution.py:51
  58.9 11.4 %all-to-all-start = ((bf16[32,56,1024]{2,1,0:T(8,128)(2,1)}), bf16[32,56,1024]{2,1,0:T(8,128)(2,1)}, u32[]{:S(2)}, u32[]{:S(2)}) async-start(bf16[32,56,1024]{2,1,0:T(8,128)(2,1)} %bitcast.41), calls=%async_computation | async-start | bytes 7340032 | tf_op jit(solution)/shard_map/all_to_all | solution.py:52
  70.3 4.3 %collective-permute-start = (bf16[1,1024,384]{2,1,0:T(8,128)(2,1)S(1)}, bf16[1,1024,384]{2,1,0:T(8,128)(2,1)S(1)}, u32[]{:S(2)}, u32[]{:S(2)}) collective-permute-start(bf16[1,1024,384]{2,1,0:T(8,128)(2,1)S(1)} %copy-done), channel_id=1, source_target_pairs={{0,16},{1,17},{2,18},{3,19},{4,20},{5,21},{6,22},{7,23},{8,24},{9,... | collective-permute-start | bytes 2359304 | tf_op jit(solution)/shard_map/ppermute | solution.py:10
  74.6 1.9 collective-permute-start.2
  76.6 4.3 %collective-permute-start.1 = (bf16[1,1024,384]{2,1,0:T(8,128)(2,1)S(1)}, bf16[1,1024,384]{2,1,0:T(8,128)(2,1)}, u32[]{:S(2)}, u32[]{:S(2)}) collective-permute-start(bf16[1,1024,384]{2,1,0:T(8,128)(2,1)S(1)} %copy-done.2), channel_id=1, source_target_pairs={{0,16},{1,17},{2,18},{3,19},{4,20},{5,21},{6,22},{7,23},{8,24},{9,... | collective-permute-start | bytes 2359304 | tf_op jit(solution)/shard_map/ppermute | solution.py:10
  80.9 0.6 dynamic_slice.3
  82.1 137.6 %collective-permute-done = bf16[1,1024,384]{2,1,0:T(8,128)(2,1)S(1)} collective-permute-done((bf16[1,1024,384]{2,1,0:T(8,128)(2,1)S(1)}, bf16[1,1024,384]{2,1,0:T(8,128)(2,1)S(1)}, u32[]{:S(2)}, u32[]{:S(2)}) %collective-permute-start) | collective-permute-done | bytes 786464 | tf_op jit(solution)/shard_map/ppermute | solution.py:10
  219.7 0.9 copy-done.6
  220.6 0.1 broadcast_select_fusion.2
  220.7 15.9 %collective-permute-done.2 = bf16[1,384,1024]{2,1,0:T(8,128)(2,1)} collective-permute-done((bf16[1,384,1024]{2,1,0:T(8,128)(2,1)S(1)}, bf16[1,384,1024]{2,1,0:T(8,128)(2,1)}, u32[]{:S(2)}, u32[]{:S(2)}) %collective-permute-start.2) | collective-permute-done | bytes 786464 | tf_op jit(solution)/shard_map/ppermute | solution.py:10
  236.8 16.7 %collective-permute-done.1 = bf16[1,1024,384]{2,1,0:T(8,128)(2,1)} collective-permute-done((bf16[1,1024,384]{2,1,0:T(8,128)(2,1)S(1)}, bf16[1,1024,384]{2,1,0:T(8,128)(2,1)}, u32[]{:S(2)}, u32[]{:S(2)}) %collective-permute-start.1) | collective-permute-done | bytes 786464 | tf_op jit(solution)/shard_map/ppermute | solution.py:10
  253.5 0.1 broadcast_select_fusion.1
  253.7 6.0 %fusion.9 = f32[1792,384]{1,0:T(8,128)} fusion(bf16[1792,1024]{1,0:T(8,128)(2,1)} %bitcast.3, bf16[1,1024,384]{2,1,0:T(8,128)(2,1)S(1)} %broadcast_select_fusion.2), kind=kOutput, calls=%fused_computation.12 | convolution fusion | flops 1409286144 | bytes 7208960 | tf_op jit(solution)/shard_map/dot_general | solution.py:14
  259.7 8.8 %convolution_convert_fusion = bf16[1792,1024]{1,0:T(8,128)(2,1)} fusion(f32[1792,384]{1,0:T(8,128)} %fusion.9, bf16[1,384,1024]{2,1,0:T(8,128)(2,1)S(1)} %broadcast_select_fusion, bf16[1792,1024]{1,0:T(8,128)(2,1)} %bitcast.3, bf16[1,1024,384]{2,1,0:T(8,128)(2,1)S(1)} %broadcast_select_fusion.1), kind=kOutput, calls=%fused_computation.4 | convolution fusion | flops 2824536064 | bytes 11665408 | tf_op jit(solution)/shard_map/dot_general | solution.py:17
  268.5 7.8 %all-to-all-start.1 = ((bf16[32,56,1024]{2,1,0:T(8,128)(2,1)}), bf16[32,56,1024]{2,1,0:T(8,128)(2,1)}, u32[]{:S(2)}, u32[]{:S(2)}) async-start(bf16[32,56,1024]{2,1,0:T(8,128)(2,1)} %bitcast.42), calls=%async_computation.1 | async-start | bytes 7340032 | tf_op jit(solution)/shard_map/all_to_all | solution.py:55
  276.4 81.8 %all-to-all-done.1 = bf16[32,56,1024]{2,1,0:T(8,128)(2,1)} async-done(((bf16[32,56,1024]{2,1,0:T(8,128)(2,1)}), bf16[32,56,1024]{2,1,0:T(8,128)(2,1)}, u32[]{:S(2)}, u32[]{:S(2)}) %all-to-all-start.1) | async-done | bytes 3670048 | tf_op jit(solution)/shard_map/all_to_all | solution.py:55
  358.3 7.5 %gather_fusion.2 = bf16[896,1024]{1,0:T(8,128)(2,1)S(1)} fusion(bf16[1792,1024]{1,0:T(8,128)(2,1)} %bitcast.9, s32[1024]{0:T(1024)S(1)} %pad_clamp_fusion.1), kind=kCustom, calls=%fused_computation.2 | custom fusion | bytes 3673600 | tf_op jit(solution)/shard_map/gather | solution.py:56
  365.8 1.8 fusion
  (38 shorter events, 0.9 us)
Async XLA Ops:
  6.3 45.8 %copy-start.7 = (bf16[112,1024]{1,0:T(8,128)(2,1)S(1)}, bf16[112,1024]{1,0:T(8,128)(2,1)}, u32[]{:S(2)}) copy-start(bf16[112,1024]{1,0:T(8,128)(2,1)} %param.8) | copy-start | bytes 688132
  58.9 11.5 %copy-start = (bf16[1,1024,384]{2,1,0:T(8,128)(2,1)S(1)}, bf16[1,1024,384]{2,1,0:T(8,128)(2,1)}, u32[]{:S(2)}) copy-start(bf16[1,1024,384]{2,1,0:T(8,128)(2,1)} %param.11) | copy-start | bytes 2359300
  58.9 15.8 %copy-start.1 = (bf16[1,384,1024]{2,1,0:T(8,128)(2,1)S(1)}, bf16[1,384,1024]{2,1,0:T(8,128)(2,1)}, u32[]{:S(2)}) copy-start(bf16[1,384,1024]{2,1,0:T(8,128)(2,1)} %param.13) | copy-start | bytes 2359300
  58.9 17.7 %copy-start.2 = (bf16[1,1024,384]{2,1,0:T(8,128)(2,1)S(1)}, bf16[1,1024,384]{2,1,0:T(8,128)(2,1)}, u32[]{:S(2)}) copy-start(bf16[1,1024,384]{2,1,0:T(8,128)(2,1)} %param.12) | copy-start | bytes 2359300
  58.9 22.0 %copy-start.9 = (s32[32]{0:T(128)S(1)}, s32[32]{0:T(128)}, u32[]{:S(2)}) copy-start(s32[32]{0:T(128)} %param.15) | copy-start | bytes 388
  58.9 194.8 %all-to-all-start = ((bf16[32,56,1024]{2,1,0:T(8,128)(2,1)}), bf16[32,56,1024]{2,1,0:T(8,128)(2,1)}, u32[]{:S(2)}, u32[]{:S(2)}) async-start(bf16[32,56,1024]{2,1,0:T(8,128)(2,1)} %bitcast.41), calls=%async_computation | async-start | bytes 7340032 | tf_op jit(solution)/shard_map/all_to_all | solution.py:52
  70.3 149.3 %collective-permute-start = (bf16[1,1024,384]{2,1,0:T(8,128)(2,1)S(1)}, bf16[1,1024,384]{2,1,0:T(8,128)(2,1)S(1)}, u32[]{:S(2)}, u32[]{:S(2)}) collective-permute-start(bf16[1,1024,384]{2,1,0:T(8,128)(2,1)S(1)} %copy-done), channel_id=1, source_target_pairs={{0,16},{1,17},{2,18},{3,19},{4,20},{5,21},{6,22},{7,23},{8,24},{9,... | collective-permute-start | bytes 2359304 | tf_op jit(solution)/shard_map/ppermute | solution.py:10
  74.6 162.0 %collective-permute-start.2 = (bf16[1,384,1024]{2,1,0:T(8,128)(2,1)S(1)}, bf16[1,384,1024]{2,1,0:T(8,128)(2,1)}, u32[]{:S(2)}, u32[]{:S(2)}) collective-permute-start(bf16[1,384,1024]{2,1,0:T(8,128)(2,1)S(1)} %copy-done.1), channel_id=1, source_target_pairs={{0,16},{1,17},{2,18},{3,19},{4,20},{5,21},{6,22},{7,23},{8,24},{9,... | collective-permute-start | bytes 2359304 | tf_op jit(solution)/shard_map/ppermute | solution.py:10
  76.6 176.9 %collective-permute-start.1 = (bf16[1,1024,384]{2,1,0:T(8,128)(2,1)S(1)}, bf16[1,1024,384]{2,1,0:T(8,128)(2,1)}, u32[]{:S(2)}, u32[]{:S(2)}) collective-permute-start(bf16[1,1024,384]{2,1,0:T(8,128)(2,1)S(1)} %copy-done.2), channel_id=1, source_target_pairs={{0,16},{1,17},{2,18},{3,19},{4,20},{5,21},{6,22},{7,23},{8,24},{9,... | collective-permute-start | bytes 2359304 | tf_op jit(solution)/shard_map/ppermute | solution.py:10
  219.7 0.9 copy-start.6
  220.7 38.9 %copy-start.3 = (bf16[1,1024,384]{2,1,0:T(8,128)(2,1)}, bf16[1,1024,384]{2,1,0:T(8,128)(2,1)S(1)}, u32[]{:S(2)}) copy-start(bf16[1,1024,384]{2,1,0:T(8,128)(2,1)S(1)} %broadcast_select_fusion.2) | copy-start | bytes 2359300
  236.8 22.9 %copy-start.4 = (bf16[1,384,1024]{2,1,0:T(8,128)(2,1)}, bf16[1,384,1024]{2,1,0:T(8,128)(2,1)S(1)}, u32[]{:S(2)}) copy-start(bf16[1,384,1024]{2,1,0:T(8,128)(2,1)S(1)} %broadcast_select_fusion) | copy-start | bytes 2359300
  253.6 6.0 %copy-start.5 = (bf16[1,1024,384]{2,1,0:T(8,128)(2,1)}, bf16[1,1024,384]{2,1,0:T(8,128)(2,1)S(1)}, u32[]{:S(2)}) copy-start(bf16[1,1024,384]{2,1,0:T(8,128)(2,1)S(1)} %broadcast_select_fusion.1) | copy-start | bytes 2359300
  268.5 7.9 %copy-start.8 = (f32[112,8]{0,1:T(8,128)S(1)}, f32[112,8]{0,1:T(8,128)}, u32[]{:S(2)}) copy-start(f32[112,8]{0,1:T(8,128)} %param.10) | copy-start | bytes 10756
  268.5 89.8 %all-to-all-start.1 = ((bf16[32,56,1024]{2,1,0:T(8,128)(2,1)}), bf16[32,56,1024]{2,1,0:T(8,128)(2,1)}, u32[]{:S(2)}, u32[]{:S(2)}) async-start(bf16[32,56,1024]{2,1,0:T(8,128)(2,1)} %bitcast.42), calls=%async_computation.1 | async-start | bytes 7340032 | tf_op jit(solution)/shard_map/all_to_all | solution.py:55
where the time goes:
time: 368 us
  waiting for transfers between devices  252 us (68%)
  local copies, waits for them, and re-layouts  64.2 us (17%)
  starting transfers between devices  29.8 us (8%)
  matrix products  14.8 us (4%)
  other arithmetic  5.32 us (1%)
    ppermute x3, waiting for transfers between devices, swapped(): return lax.ppermute(value, axis, pairs)  170 us
    all_to_all x1, waiting for transfers between devices, per_device(): lax.all_to_all(computed, 'expert', split_axis=0, concat_axis=0, tiled=True)  81.8 us
    scatter x1, local copies, waits for them, and re-layouts, per_device(): jnp.full((count_dev, capacity), tok_rows, jnp.int32).at[target, slot_index]  45.7 us
    all_to_all x1, starting transfers between devices, per_device(): lax.all_to_all(outgoing, 'expert', split_axis=0, concat_axis=0, tiled=True)  11.4 us
    ppermute x3, starting transfers between devices, swapped(): return lax.ppermute(value, axis, pairs)  10.5 us
    dot_general x1, matrix products, expert_apply(): jnp.dot(hidden, down_w, preferred_element_type=jnp.float32)  8.83 us
    all_to_all x1, starting transfers between devices, per_device(): lax.all_to_all(computed, 'expert', split_axis=0, concat_axis=0, tiled=True)  7.84 us
    gather x1, local copies, waits for them, and re-layouts, per_device(): picked_rows = returned.reshape(-1, width)[target * capacity + slot_index]  7.51 us
  transfers between devices with their start and end apart: 5, of which 4 were waited for; matrix products, arithmetic and copies ran while one was open for 0% of the time, Pallas kernels for 0%

commit v1 on v0

v1 whole, which is shorter than its diff:
```python
import jax
import jax.numpy as jnp
from jax import lax
from jax.experimental import pallas as pl
from jax.experimental.pallas import tpu as pltpu
from jax.sharding import PartitionSpec as P

MESH = pl.DeviceIdType.MESH
F32 = jnp.float32
BF16 = jnp.bfloat16


class Links:
    def __init__(self, send, recv):
        self.send, self.recv, self.count, self.started = send, recv, 0, []

    def new(self):
        self.count += 1
        return self.count - 1

    def copy(self, k, src, dst, dev):
        return pltpu.make_async_remote_copy(
            src_ref=src,
            dst_ref=dst,
            send_sem=self.send.at[k],
            recv_sem=self.recv.at[k],
            device_id=dev,
            device_id_type=MESH,
        )

    def start(self, k, src, dst, dev):
        c = self.copy(k, src, dst, dev)
        c.start()
        self.started.append(c)

    def arrived(self, k, dst, dev):
        self.copy(k, dst, dst, dev).wait_recv()

    def finish(self):
        for c in self.started:
            c.wait_send()


def kernel(
    tok_ref, table_ref, flag_ref, wg_hbm, wu_hbm, wd_hbm,
    mixed_ref, sg_hbm, su_hbm, sd_hbm,
    x_buf, meta, gcol, wgu, wdn, hid, acc, sendb, half_in, full_in, z_in,
    sel_g, sel_u, sel_d, send_sem, recv_sem, local_sem,
):
    rows, width = tok_ref.shape
    ff = wg_hbm.shape[1]
    half = width // 2
    dp = lax.axis_index("dp")
    ex = lax.axis_index("expert")
    zh, y = dp // 4, dp % 4
    zl, x, c = ex // 8, (ex // 2) % 4, ex % 2
    zo = zl + 1 - 2 * (zl % 2)

    def at(dx, other):
        return {"dp": dp, "expert": ((zo if other else zl) * 4 + (x + dx + 4) % 4) * 2 + c}

    def at_z(d):
        zz = (zh * 4 + zl + d + 16) % 16
        return {"dp": (zz // 4) * 4 + y, "expert": ((zz % 4) * 4 + x) * 2 + c}

    def at_y(d):
        return {"dp": zh * 4 + (y + d + 4) % 4, "expert": ex}

    sibling = {"dp": dp, "expert": ex + 1 - 2 * c}
    xr, xl, zp = at(1, False), at(-1, False), at(0, True)
    peers = [at(1, False), at(-1, False), at(2, False), at(0, True), at(1, True), at(-1, True), at(2, True)]
    partners = peers + [at_z(2), at_z(-2), at_y(1), at_y(-1), sibling]

    barrier = pltpu.get_barrier_semaphore()
    for dev in partners:
        pl.semaphore_signal(barrier, inc=1, device_id=dev, device_id_type=MESH)

    own_copies = [
        pltpu.make_async_copy(wg_hbm, wgu.at[0, :, pl.ds(0, ff)], local_sem.at[0]),
        pltpu.make_async_copy(wu_hbm, wgu.at[0, :, pl.ds(ff, ff)], local_sem.at[1]),
        pltpu.make_async_copy(wd_hbm, wdn.at[0], local_sem.at[2]),
    ]
    for cp in own_copies:
        cp.start()
    pl.semaphore_wait(barrier, len(partners))

    link = Links(send_sem, recv_sem)

    def part(a, slot, qi, h):
        n = wd_hbm.shape[0] // 4 if a == 2 else width // 4
        start, size = qi * n, n
        if h is not None:
            start, size = start + h * (n // 2), n // 2
        start = pl.multiple_of(start, 16)
        if a == 2:
            return wdn.at[slot, pl.ds(start, size), :]
        return wgu.at[slot, pl.ds(start, size), pl.ds(a * ff, ff)]

    def own_part(a, qi, h):
        ref = (wg_hbm, wu_hbm, wd_hbm)[a]
        n = ref.shape[0] // 4
        return ref.at[pl.ds(pl.multiple_of(qi * n + h * (n // 2), 16), n // 2), :]

    zk = {}
    for a in range(3):
        for h in range(2):
            zk[a, h] = link.new()
            link.start(zk[a, h], own_part(a, y, h), part(a, 2, y, h), at_z(2 if h == 0 else -2))
    mk = []
    slots = [(3, 0), (1, 0), (2, 0), (0, 1), (3, 1), (1, 1), (2, 1)]
    targets = [(1, 0), (3, 0), (2, 0), (0, 1), (1, 1), (3, 1), (2, 1)]
    for i, dev in enumerate(peers):
        mk.append(link.new())
        dx, dz = targets[i]
        sx, sz = slots[i]
        link.start(mk[i], table_ref.at[dx * 2 + dz], meta.at[sx * 2 + sz], dev)
    kz, kr, kl = link.new(), link.new(), link.new()
    link.start(kz, tok_ref, x_buf.at[0, pl.ds(rows, rows)], zp)
    link.start(kr, tok_ref, x_buf.at[3, pl.ds(0, rows)], xr)
    link.start(kl, tok_ref, x_buf.at[1, pl.ds(0, rows)], xl)
    ck = []
    for a, ref in enumerate((wg_hbm, wu_hbm, wd_hbm)):
        ck.append(link.new())
        dst = wdn.at[1] if a == 2 else wgu.at[1, :, pl.ds(a * ff, ff)]
        link.start(ck[a], ref, dst, sibling)
    x_buf[0, 0:rows, :] = tok_ref[...]
    meta[0] = table_ref[0]

    kr1, kl1 = link.new(), link.new()
    link.arrived(kz, x_buf.at[0, pl.ds(rows, rows)], zp)
    link.start(kr1, x_buf.at[0, pl.ds(rows, rows)], x_buf.at[3, pl.ds(rows, rows)], xr)
    link.start(kl1, x_buf.at[0, pl.ds(rows, rows)], x_buf.at[1, pl.ds(rows, rows)], xl)
    fr, fl = {}, {}

    def forward(dz, got_l, got_r):
        r = pl.ds(dz * rows, rows)
        fr[dz], fl[dz] = link.new(), link.new()
        link.arrived(got_l, x_buf.at[3, r], xl)
        link.start(fr[dz], x_buf.at[3, r, pl.ds(0, half)], x_buf.at[2, r, pl.ds(0, half)], xr)
        link.arrived(got_r, x_buf.at[1, r], xr)
        link.start(fl[dz], x_buf.at[1, r, pl.ds(half, half)], x_buf.at[2, r, pl.ds(half, half)], xl)

    forward(0, kr, kl)

    up, down = at_y(1), at_y(-1)
    yk = {}

    def spread(a):
        for h in range(2):
            link.arrived(zk[a, h], part(a, 2, y, h), at_z(-2 if h == 0 else 2))
        for h in range(2):
            for d in (1, -1):
                yk[a, h, d] = link.new()
                link.start(yk[a, h, d], part(a, 2, y, h), part(a, 2, y, h), up if d == 1 else down)
        share(a, y)

    share_k = []

    def share(a, qi):
        k = link.new()
        link.start(k, part(a, 2, qi, None), part(a, 3, qi, None), sibling)
        share_k.append((k, a, qi))

    yp, ym, yo = (y + 1) % 4, (y + 3) % 4, (y + 2) % 4
    fk = {}

    def relay(a):
        link.arrived(yk[a, 0, 1], part(a, 2, ym, 0), down)
        fk[a, 0] = link.new()
        link.start(fk[a, 0], part(a, 2, ym, 0), part(a, 2, ym, 0), up)
        link.arrived(yk[a, 1, -1], part(a, 2, yp, 1), up)
        fk[a, 1] = link.new()
        link.start(fk[a, 1], part(a, 2, yp, 1), part(a, 2, yp, 1), down)
        link.arrived(yk[a, 1, 1], part(a, 2, ym, 1), down)
        link.arrived(yk[a, 0, -1], part(a, 2, yp, 0), up)
        share(a, ym)
        share(a, yp)

    def last(a):
        link.arrived(fk[a, 0], part(a, 2, yo, 0), down)
        link.arrived(fk[a, 1], part(a, 2, yo, 1), up)
        share(a, yo)

    def ffn(dx, base):
        xv = x_buf[dx]
        gates = gcol[dx]
        for j in range(2):
            r = jnp.dot(xv, wgu[base + j], preferred_element_type=F32)
            g, u = r[:, :ff], r[:, ff:]
            s = (0.5 * g) * (1.0 + jnp.tanh(0.5 * g))
            hid[:, j * ff : (j + 1) * ff] = (s * u * gates[:, base + j : base + j + 1]).astype(BF16)

    def first_half(dx):
        ffn(dx, 0)
        w = wdn[0:2].reshape(2 * ff, width)
        acc[dx] = jnp.dot(hid[...], w, preferred_element_type=F32)

    def second_half(dx):
        ffn(dx, 2)
        w = wdn[2:4].reshape(2 * ff, width)
        return acc[dx] + jnp.dot(hid[...], w, preferred_element_type=F32)

    for a in range(3):
        spread(a)
    for i in range(7):
        sx, sz = slots[i]
        link.arrived(mk[i], meta.at[sx * 2 + sz], peers[i])
    for dx in range(4):
        for dz in range(2):
            gcol[dx, dz * rows : (dz + 1) * rows, :] = meta[dx * 2 + dz].T[:rows, :]
    for cp in own_copies:
        cp.wait()
    for a in range(3):
        link.arrived(ck[a], wdn.at[1] if a == 2 else wgu.at[1, :, pl.ds(a * ff, ff)], sibling)
    forward(1, kr1, kl1)
    first_half(0)
    relay(0)
    first_half(1)
    relay(1)
    first_half(3)
    relay(2)
    last(0)
    for dz in range(2):
        r = pl.ds(dz * rows, rows)
        link.arrived(fr[dz], x_buf.at[2, r, pl.ds(0, half)], xl)
        link.arrived(fl[dz], x_buf.at[2, r, pl.ds(half, half)], xr)
    first_half(2)
    last(1)
    last(2)

    for k, a, qi in share_k:
        link.arrived(k, part(a, 3, qi, None), sibling)

    low, high = pl.ds(0, half), pl.ds(half, half)
    p2 = second_half(2)
    sendb[2] = p2.astype(BF16)
    hr, hl, gr, gl = {}, {}, {}, {}
    for dz in (1, 0):
        r = pl.ds(dz * rows, rows)
        hr[dz], hl[dz] = link.new(), link.new()
        link.start(hr[dz], sendb.at[2, r, low], half_in.at[0, r], xr)
        link.start(hl[dz], sendb.at[2, r, high], half_in.at[1, r], xl)
    acc[1] = second_half(1)
    acc[3] = second_half(3)
    for dz in (1, 0):
        r, rs = pl.ds(dz * rows, rows), slice(dz * rows, (dz + 1) * rows)
        gr[dz], gl[dz] = link.new(), link.new()
        link.arrived(hr[dz], half_in.at[0, r], xl)
        sendb[1, rs, :half] = (acc[1, rs, :half] + half_in[0, rs].astype(F32)).astype(BF16)
        sendb[1, rs, half:] = acc[1, rs, half:].astype(BF16)
        link.start(gr[dz], sendb.at[1, r], full_in.at[0, r], xr)
        link.arrived(hl[dz], half_in.at[1, r], xr)
        sendb[3, rs, half:] = (acc[3, rs, half:] + half_in[1, rs].astype(F32)).astype(BF16)
        sendb[3, rs, :half] = acc[3, rs, :half].astype(BF16)
        link.start(gl[dz], sendb.at[3, r], full_in.at[1, r], xl)

    taken = flag_ref[0:1, 0:1] == 1
    sel_g[...] = jnp.where(taken, wgu[2, :, :ff], wgu[0, :, :ff])
    sel_u[...] = jnp.where(taken, wgu[2, :, ff:], wgu[0, :, ff:])
    sel_d[...] = jnp.where(taken, wdn[2], wdn[0])
    out_copies = [
        pltpu.make_async_copy(sel_g, sg_hbm, local_sem.at[3]),
        pltpu.make_async_copy(sel_u, su_hbm, local_sem.at[4]),
        pltpu.make_async_copy(sel_d, sd_hbm, local_sem.at[5]),
    ]
    for cp in out_copies:
        cp.start()

    acc[0] = second_half(0)
    kz2 = link.new()
    rz, r0 = pl.ds(rows, rows), pl.ds(0, rows)
    link.arrived(gr[1], full_in.at[0, rz], xl)
    link.arrived(gl[1], full_in.at[1, rz], xr)
    sendb[0, rows:, :] = (acc[0, rows:, :] + full_in[0, rows:].astype(F32) + full_in[1, rows:].astype(F32)).astype(BF16)
    link.start(kz2, sendb.at[0, rz], z_in, zp)
    link.arrived(gr[0], full_in.at[0, r0], xl)
    link.arrived(gl[0], full_in.at[1, r0], xr)
    total = acc[0, :rows, :] + full_in[0, :rows].astype(F32) + full_in[1, :rows].astype(F32)
    link.arrived(kz2, z_in, zp)
    mixed_ref[...] = (total + z_in[...].astype(F32)).astype(BF16)
    link.finish()
    for cp in out_copies:
        cp.wait()


def per_device(tokens, expert_ids, gate_probs, w_gate, w_up, w_down, placement, swap_flags):
    rows, width = tokens.shape
    ff = w_gate.shape[2]
    ex = lax.axis_index("expert")
    zl, x, c = ex // 8, (ex // 2) % 4, ex % 2
    dx, dz, j = jnp.meshgrid(jnp.arange(4), jnp.arange(2), jnp.arange(4), indexing="ij")
    zt = jnp.where(dz == 1, jnp.bitwise_xor(zl, 1), zl)
    zt = jnp.where(j >= 2, jnp.bitwise_xor(zt, 2), zt)
    dev = (zt * 4 + (x + dx) % 4) * 2 + jnp.where(j % 2 == 1, 1 - c, c)
    wanted = placement[dev.reshape(-1)]
    ids = expert_ids.T
    probs = gate_probs.T
    table = jnp.sum(jnp.where(ids[None] == wanted[:, None, None], probs[None], 0.0), axis=1)
    table = table.reshape(8, 4, rows)
    table = jnp.pad(table, ((0, 0), (0, 4), (0, 128 - rows)))
    flag = jnp.broadcast_to(swap_flags[ex], (8, 128))

    vmem = pl.BlockSpec(memory_space=pltpu.VMEM)
    hbm = pl.BlockSpec(memory_space=pl.ANY)
    mixed, sg, su, sd = pl.pallas_call(
        kernel,
        out_shape=(
            jax.ShapeDtypeStruct((rows, width), BF16),
            jax.ShapeDtypeStruct((width, ff), BF16),
            jax.ShapeDtypeStruct((width, ff), BF16),
            jax.ShapeDtypeStruct((ff, width), BF16),
        ),
        in_specs=[vmem, vmem, vmem, hbm, hbm, hbm],
        out_specs=(vmem, hbm, hbm, hbm),
        scratch_shapes=[
            pltpu.VMEM((4, 2 * rows, width), BF16),
            pltpu.VMEM((8, 8, 128), F32),
            pltpu.VMEM((4, 2 * rows, 8), F32),
            pltpu.VMEM((4, width, 2 * ff), BF16),
            pltpu.VMEM((4, ff, width), BF16),
            pltpu.VMEM((2 * rows, 2 * ff), BF16),
            pltpu.VMEM((4, 2 * rows, width), F32),
            pltpu.VMEM((4, 2 * rows, width), BF16),
            pltpu.VMEM((2, 2 * rows, width // 2), BF16),
            pltpu.VMEM((2, 2 * rows, width), BF16),
            pltpu.VMEM((rows, width), BF16),
            pltpu.VMEM((width, ff), BF16),
            pltpu.VMEM((width, ff), BF16),
            pltpu.VMEM((ff, width), BF16),
            pltpu.SemaphoreType.DMA((80,)),
            pltpu.SemaphoreType.DMA((80,)),
            pltpu.SemaphoreType.DMA((6,)),
        ],
        compiler_params=pltpu.CompilerParams(
            collective_id=0, has_side_effects=True, vmem_limit_bytes=48 * 2**20
        ),
    )(tokens, table, flag, w_gate[0], w_up[0], w_down[0])
    return mixed, sg[None], su[None], sd[None]


def solution(mesh):
    in_specs = (
        P(("dp", "expert"), None),
        P(("dp", "expert"), None),
        P(("dp", "expert"), None),
        P("expert", None, None),
        P("expert", None, None),
        P("expert", None, None),
        P(),
        P(),
    )
    out_specs = (
        P(("dp", "expert"), None),
        P(("dp", "expert"), None, None),
        P(("dp", "expert"), None, None),
        P(("dp", "expert"), None, None),
    )
    return jax.shard_map(
        per_device, mesh=mesh, in_specs=in_specs, out_specs=out_specs, check_vma=False
    )
```

time: 368 us -> 88.2 us (0.24)
  waiting for transfers between devices: 252 us -> 0 us
  Pallas kernels: 0 us -> 77.1 us
  local copies, waits for them, and re-layouts: 64.2 us -> 9.91 us
  starting transfers between devices: 29.8 us -> 0 us
  matrix products: 14.8 us -> 0 us
  other arithmetic: 5.32 us -> 0.17 us
    ppermute x3 -> x0, waiting for transfers between devices: 170 us -> none  [swapped(): return lax.ppermute(value, axis, pairs)]
    all_to_all x2 -> x0, waiting for transfers between devices: 81.8 us -> none  [the longest x1 81.8 us: per_device(): lax.all_to_all(computed, 'expert', split_axis=0, concat_axis=0, tiled=True)]
    pallas_call x0 -> x1, Pallas kernels: none -> 77.1 us  [per_device(): pl.pallas_call(kernel, out_shape=(jax.ShapeDtypeStruct((rows, width), BF1...]
    scatter x1 -> x0, local copies, waits for them, and re-layouts: 45.7 us -> none  [per_device(): jnp.full((count_dev, capacity), tok_rows, jnp.int32).at[target, slot_index]]
    all_to_all x2 -> x0, starting transfers between devices: 19.3 us -> none  [the longest x1 11.4 us: per_device(): lax.all_to_all(outgoing, 'expert', split_axis=0, concat_axis=0, tiled=True)]
    gather x3 -> x1, local copies, waits for them, and re-layouts: 15.5 us -> 0.7 us  [per_device(): wanted = placement[dev.reshape(-1)]]
    dot_general x2 -> x0, matrix products: 14.8 us -> none  [the longest x1 8.83 us: expert_apply(): jnp.dot(hidden, down_w, preferred_element_type=jnp.float32)]
    ppermute x3 -> x0, starting transfers between devices: 10.5 us -> none  [swapped(): return lax.ppermute(value, axis, pairs)]
  transfers between devices with their start and end apart: 5 -> 0, of which waited for: 4 -> 0; matrix products, arithmetic and copies ran while one was open for 0% -> 0% of each run, Pallas kernels for 0% -> 0%
where the time goes in v1:
time: 88.2 us; the launch traced here: 88 us
  Pallas kernels  77.1 us (87%)
  local copies, waits for them, and re-layouts  9.91 us (11%)
    pallas_call x1, Pallas kernels, per_device(): pl.pallas_call(kernel, out_shape=(jax.ShapeDtypeStruct((rows, width), BF1...  77.1 us
    unnamed x20, local copies, waits for them, and re-layouts  7.48 us

profile of v1, /device:TPU:1, one launch (start us, length us, event | category | flops | bytes accessed | tf_op | source)
XLA Modules:
  0.0 88.0 jit_solution(10191357526542959486)
XLA Ops:
  0.6 0.0 copy-start
  0.7 0.0 copy-start.7
  0.7 0.6 copy-done.7
  1.4 0.6 dynamic_slice.3
  2.0 0.1 select_n.114
  2.1 0.1 broadcast_in_dim.62
  2.2 0.7 broadcast_in_dim.75.flag_ref
  2.8 0.1 broadcast_in_dim.66
  2.9 0.1 broadcast_in_dim.67
  3.0 0.1 broadcast_in_dim.65
  3.0 0.1 select_n.106
  3.2 0.0 copy-start.6
  3.2 0.0 copy-start.4
  3.2 0.7 gather_fusion
  3.9 0.1 select_reduce_fusion
  4.1 0.1 copy-done.4
  4.2 1.1 %copy-done.1 = bf16[1,1024,384]{2,1,0:T(8,128)(2,1)S(1)} copy-done((bf16[1,1024,384]{2,1,0:T(8,128)(2,1)S(1)}, bf16[1,1024,384]{2,1,0:T(8,128)(2,1)}, u32[]{:S(2)}) %copy-start.1) | copy-done | bytes 786456
  5.3 1.1 %copy-done.2 = bf16[1,1024,384]{2,1,0:T(8,128)(2,1)S(1)} copy-done((bf16[1,1024,384]{2,1,0:T(8,128)(2,1)S(1)}, bf16[1,1024,384]{2,1,0:T(8,128)(2,1)}, u32[]{:S(2)}) %copy-start.2) | copy-done | bytes 786456
  6.4 1.1 %copy-done.3 = bf16[1,384,1024]{2,1,0:T(8,128)(2,1)S(1)} copy-done((bf16[1,384,1024]{2,1,0:T(8,128)(2,1)S(1)}, bf16[1,384,1024]{2,1,0:T(8,128)(2,1)}, u32[]{:S(2)}) %copy-start.3) | copy-done | bytes 786456
  7.6 77.1 %shard_map.111 = (bf16[112,1024]{1,0:T(8,128)(2,1)S(1)}, bf16[1024,384]{1,0:T(8,128)(2,1)S(1)}, bf16[1024,384]{1,0:T(8,128)(2,1)S(1)}, bf16[384,1024]{1,0:T(8,128)(2,1)S(1)}) custom-call(bf16[112,1024]{1,0:T(8,128)(2,1)S(1)} %copy-done.4, f32[8,8,128]{2,1,0:T(8,128)S(1)} %pad.4.table_ref, s32[8,128]{1,0:T(8,128)S(1)} %broadcast_in_dim.75.flag_ref, ...), custom_call_target="tpu_custom_call" | custom-call | tf_op jit(solution)/shard_map/pallas_call | solution.py:305
  84.6 0.7 copy.16
  85.3 0.9 copy.17
  86.2 0.9 copy.18
  87.1 0.9 copy.19
  (17 shorter events, 0.1 us)
Async XLA Ops:
  0.6 2.5 %copy-start = (s32[32]{0:T(128)S(1)}, s32[32]{0:T(128)}, u32[]{:S(2)}) copy-start(s32[32]{0:T(128)} %param.14) | copy-start | bytes 388
  0.7 0.7 copy-start.7
  3.2 0.7 copy-start.5
  3.2 0.7 copy-start.6
  3.2 0.9 %copy-start.4 = (bf16[112,1024]{1,0:T(8,128)(2,1)S(1)}, bf16[112,1024]{1,0:T(8,128)(2,1)}, u32[]{:S(2)}) copy-start(bf16[112,1024]{1,0:T(8,128)(2,1)} %tok_ref.1) | copy-start | bytes 688132
  4.2 1.1 %copy-start.1 = (bf16[1,1024,384]{2,1,0:T(8,128)(2,1)S(1)}, bf16[1,1024,384]{2,1,0:T(8,128)(2,1)}, u32[]{:S(2)}) copy-start(bf16[1,1024,384]{2,1,0:T(8,128)(2,1)} %param.11) | copy-start | bytes 2359300
  5.3 1.1 %copy-start.2 = (bf16[1,1024,384]{2,1,0:T(8,128)(2,1)S(1)}, bf16[1,1024,384]{2,1,0:T(8,128)(2,1)}, u32[]{:S(2)}) copy-start(bf16[1,1024,384]{2,1,0:T(8,128)(2,1)} %param.12) | copy-start | bytes 2359300
  6.4 1.1 %copy-start.3 = (bf16[1,384,1024]{2,1,0:T(8,128)(2,1)S(1)}, bf16[1,384,1024]{2,1,0:T(8,128)(2,1)}, u32[]{:S(2)}) copy-start(bf16[1,384,1024]{2,1,0:T(8,128)(2,1)} %param.13) | copy-start | bytes 2359300

commit v2 on v1

v2 whole, which is shorter than its diff:
```python
import jax
import jax.numpy as jnp
from jax import lax
from jax.experimental import pallas as pl
from jax.experimental.pallas import tpu as pltpu
from jax.sharding import PartitionSpec as P

MESH = pl.DeviceIdType.MESH
F32 = jnp.float32
BF16 = jnp.bfloat16


class Links:
    def __init__(self, send, recv):
        self.send, self.recv, self.count, self.started = send, recv, 0, []

    def new(self):
        self.count += 1
        return self.count - 1

    def copy(self, k, src, dst, dev):
        return pltpu.make_async_remote_copy(
            src_ref=src,
            dst_ref=dst,
            send_sem=self.send.at[k],
            recv_sem=self.recv.at[k],
            device_id=dev,
            device_id_type=MESH,
        )

    def start(self, k, src, dst, dev):
        c = self.copy(k, src, dst, dev)
        c.start()
        self.started.append(c)

    def arrived(self, k, dst, dev):
        self.copy(k, dst, dst, dev).wait_recv()

    def finish(self):
        for c in self.started:
            c.wait_send()


def kernel(
    ids_ref, prob_ref, flag_ref, place_ref, tok_hbm, wg_hbm, wu_hbm, wd_hbm,
    mixed_ref, sg_ref, su_ref, sd_ref,
    x_buf, flip, table_ref, meta, gcol, wgu, wdn, hid, acc, sendb, half_in, full_in, z_in,
    send_sem, recv_sem, local_sem,
):
    rows, width = tok_hbm.shape
    ff = wg_hbm.shape[1]
    half = width // 2
    dp = lax.axis_index("dp")
    ex = lax.axis_index("expert")
    zh, y = dp // 4, dp % 4
    zl, x, c = ex // 8, (ex // 2) % 4, ex % 2
    zo = zl + 1 - 2 * (zl % 2)

    def at(dx, other):
        return {"dp": dp, "expert": ((zo if other else zl) * 4 + (x + dx + 4) % 4) * 2 + c}

    def at_z(d):
        zz = (zh * 4 + zl + d + 16) % 16
        return {"dp": (zz // 4) * 4 + y, "expert": ((zz % 4) * 4 + x) * 2 + c}

    def at_y(d):
        return {"dp": zh * 4 + (y + d + 4) % 4, "expert": ex}

    sibling = {"dp": dp, "expert": ex + 1 - 2 * c}
    xr, xl, zp = at(1, False), at(-1, False), at(0, True)
    peers = [at(1, False), at(-1, False), at(2, False), at(0, True), at(1, True), at(-1, True), at(2, True)]
    partners = peers + [at_z(2), at_z(-2), at_y(1), at_y(-1), sibling]

    barrier = pltpu.get_barrier_semaphore()
    for dev in partners:
        pl.semaphore_signal(barrier, inc=1, device_id=dev, device_id_type=MESH)

    own_copies = [
        pltpu.make_async_copy(wg_hbm, wgu.at[0, :, pl.ds(0, ff)], local_sem.at[0]),
        pltpu.make_async_copy(wu_hbm, wgu.at[0, :, pl.ds(ff, ff)], local_sem.at[1]),
        pltpu.make_async_copy(wd_hbm, wdn.at[0], local_sem.at[2]),
    ]
    own_tokens = pltpu.make_async_copy(tok_hbm, x_buf.at[0, pl.ds(0, rows)], local_sem.at[3])
    own_tokens.start()
    for cp in own_copies:
        cp.start()

    flip[...] = jnp.zeros_like(flip)
    flip[0, :, 0:rows] = ids_ref[...].astype(F32)
    flip[1, :, 0:rows] = prob_ref[...]
    ids_t, prob_t = flip[0], flip[1]
    for dx in range(4):
        for dz in range(2):
            zt = zo if dz else zl
            for j in range(4):
                zj = (zt + 2) % 4 if j >= 2 else zt
                cj = 1 - c if j % 2 else c
                e = place_ref[(zj * 4 + (x + dx) % 4) * 2 + cj].astype(F32)
                hit = jnp.where(ids_t == e, prob_t, 0.0)
                table_ref[dx * 2 + dz, j : j + 1, :] = jnp.sum(hit, axis=0, keepdims=True)
            table_ref[dx * 2 + dz, 4:8, :] = jnp.zeros((4, 128), F32)
    pl.semaphore_wait(barrier, len(partners))

    link = Links(send_sem, recv_sem)

    pieces = [(0, 0, 128), (0, 128, ff - 128), (1, 0, ff), (2, 0, half), (2, half, half // 2), (2, half + half // 2, half // 2)]

    def row_range(i, qi, h):
        n = (wd_hbm.shape[0] if i == 2 else width) // 4
        start, size = qi * n, n
        if h is not None:
            start, size = start + h * (n // 2), n // 2
        return pl.ds(pl.multiple_of(start, 16), size)

    def part(a, slot, qi, h):
        i, c0, cn = pieces[a]
        r = row_range(i, qi, h)
        if i == 2:
            return wdn.at[slot, r, pl.ds(c0, cn)]
        return wgu.at[slot, r, pl.ds(i * ff + c0, cn)]

    def own_part(a, qi, h):
        i, c0, cn = pieces[a]
        return (wg_hbm, wu_hbm, wd_hbm)[i].at[row_range(i, qi, h), pl.ds(c0, cn)]

    yp, ym, yo = (y + 1) % 4, (y + 3) % 4, (y + 2) % 4
    direct = -1

    zk, ok = {}, {}

    def fetch(a):
        for h in range(2):
            zk[a, h] = link.new()
            link.start(zk[a, h], own_part(a, y, h), part(a, 2, y, h), at_z(2 if h == 0 else -2))

    def fetch_opposite(a):
        for h in range(2):
            ok[a, h] = link.new()
            link.start(ok[a, h], own_part(a, yo, h), part(a, 2, yo, h), at_z(2 if h == 0 else -2))

    mk = []
    slots = [(3, 0), (1, 0), (2, 0), (0, 1), (3, 1), (1, 1), (2, 1)]
    targets = [(1, 0), (3, 0), (2, 0), (0, 1), (1, 1), (3, 1), (2, 1)]

    def tables():
        for i, dev in enumerate(peers):
            mk.append(link.new())
            dx, dz = targets[i]
            sx, sz = slots[i]
            link.start(mk[i], table_ref.at[dx * 2 + dz], meta.at[sx * 2 + sz], dev)

    def tables_here():
        for i in range(7):
            sx, sz = slots[i]
            link.arrived(mk[i], meta.at[sx * 2 + sz], peers[i])
        meta[0] = table_ref[0]
        for dx in range(4):
            for dz in range(2):
                gcol[dx, dz * rows : (dz + 1) * rows, :] = meta[dx * 2 + dz].T[:rows, :]

    kz, kr, kl, kf = {}, {}, {}, {}

    def tok(dx, dz, h):
        return x_buf.at[dx, pl.ds(dz * rows, rows), pl.ds(h * half, half)]

    def pair(h):
        kz[h] = link.new()
        link.start(kz[h], tok_hbm.at[:, pl.ds(h * half, half)], tok(0, 1, h), zp)

    def around(dz, h):
        if dz == 1:
            link.arrived(kz[h], tok(0, 1, h), zp)
        src = tok(0, 1, h) if dz else tok_hbm.at[:, pl.ds(h * half, half)]
        kr[dz, h], kl[dz, h] = link.new(), link.new()
        link.start(kr[dz, h], src, tok(3, dz, h), xr)
        link.start(kl[dz, h], src, tok(1, dz, h), xl)

    def forward(dz, h):
        kf[dz, h] = link.new()
        if h == 0:
            link.arrived(kr[dz, 0], tok(3, dz, 0), xl)
            link.start(kf[dz, 0], tok(3, dz, 0), tok(2, dz, 0), xr)
        else:
            link.arrived(kl[dz, 1], tok(1, dz, 1), xr)
            link.start(kf[dz, 1], tok(1, dz, 1), tok(2, dz, 1), xl)

    def near(dx):
        for dz in range(2):
            if dx == 3:
                link.arrived(kr[dz, 1], tok(3, dz, 1), xl)
            else:
                link.arrived(kl[dz, 0], tok(1, dz, 0), xr)

    def far():
        for dz in range(2):
            link.arrived(kf[dz, 0], tok(2, dz, 0), xl)
            link.arrived(kf[dz, 1], tok(2, dz, 1), xr)

    ck = []

    def own_weights():
        for a, ref in enumerate((wg_hbm, wu_hbm, wd_hbm)):
            ck.append(link.new())
            dst = wdn.at[1] if a == 2 else wgu.at[1, :, pl.ds(a * ff, ff)]
            link.start(ck[a], ref, dst, sibling)

    def own_weights_here():
        for cp in own_copies + [own_tokens]:
            cp.wait()
        for a in range(3):
            link.arrived(ck[a], wdn.at[1] if a == 2 else wgu.at[1, :, pl.ds(a * ff, ff)], sibling)

    up, down = at_y(1), at_y(-1)
    yk = {}

    def spread(a):
        for h in range(2):
            link.arrived(zk[a, h], part(a, 2, y, h), at_z(-2 if h == 0 else 2))
        for h in range(2):
            for d in (1, -1):
                yk[a, h, d] = link.new()
                link.start(yk[a, h, d], part(a, 2, y, h), part(a, 2, y, h), up if d == 1 else down)
        share(a, y)

    share_k = {}

    def share(a, qi):
        k = link.new()
        link.start(k, part(a, 2, qi, None), part(a, 3, qi, None), sibling)
        share_k.setdefault(a, []).append((k, qi))

    fk = {}

    def relay(a):
        link.arrived(yk[a, 0, 1], part(a, 2, ym, 0), down)
        if a != direct:
            fk[a, 0] = link.new()
            link.start(fk[a, 0], part(a, 2, ym, 0), part(a, 2, ym, 0), up)
        link.arrived(yk[a, 1, -1], part(a, 2, yp, 1), up)
        if a != direct:
            fk[a, 1] = link.new()
            link.start(fk[a, 1], part(a, 2, yp, 1), part(a, 2, yp, 1), down)
        link.arrived(yk[a, 1, 1], part(a, 2, ym, 1), down)
        share(a, ym)
        link.arrived(yk[a, 0, -1], part(a, 2, yp, 0), up)
        share(a, yp)

    def last(a):
        if a == direct:
            link.arrived(ok[a, 0], part(a, 2, yo, 0), at_z(-2))
            link.arrived(ok[a, 1], part(a, 2, yo, 1), at_z(2))
        else:
            link.arrived(fk[a, 0], part(a, 2, yo, 0), down)
            link.arrived(fk[a, 1], part(a, 2, yo, 1), up)
        share(a, yo)

    def shared(a):
        for k, qi in share_k[a]:
            link.arrived(k, part(a, 3, qi, None), sibling)

    def ffn(dx, base, hid):
        xv = x_buf[dx]
        gates = gcol[dx]
        for j in range(2):
            r = jnp.dot(xv, wgu[base + j], preferred_element_type=F32)
            g, u = r[:, :ff], r[:, ff:]
            s = (0.5 * g) * (1.0 + jnp.tanh(0.5 * g))
            hid[:, j * ff : (j + 1) * ff] = (s * u * gates[:, base + j : base + j + 1]).astype(BF16)

    def first_half(dx):
        ffn(dx, 0, hid.at[dx])
        w = wdn[0:2].reshape(2 * ff, width)
        acc[dx] = jnp.dot(hid[dx], w, preferred_element_type=F32)

    def second_half(dx):
        w = wdn[2:4].reshape(2 * ff, width)
        return acc[dx] + jnp.dot(hid[dx], w, preferred_element_type=F32)

    hr, hl, gr, gl = {}, {}, {}, {}
    low, high = pl.ds(0, half), pl.ds(half, half)

    def send_far():
        sendb[2] = second_half(2).astype(BF16)
        for dz in (1, 0):
            r = pl.ds(dz * rows, rows)
            hr[dz], hl[dz] = link.new(), link.new()
            link.start(hr[dz], sendb.at[2, r, low], half_in.at[0, r], xr)
            link.start(hl[dz], sendb.at[2, r, high], half_in.at[1, r], xl)

    def send_near(dz):
        r, rs = pl.ds(dz * rows, rows), slice(dz * rows, (dz + 1) * rows)
        gr[dz], gl[dz] = link.new(), link.new()
        link.arrived(hr[dz], half_in.at[0, r], xl)
        sendb[1, rs, :half] = (acc[1, rs, :half] + half_in[0, rs].astype(F32)).astype(BF16)
        sendb[1, rs, half:] = acc[1, rs, half:].astype(BF16)
        link.start(gr[dz], sendb.at[1, r], full_in.at[0, r], xr)
        link.arrived(hl[dz], half_in.at[1, r], xr)
        sendb[3, rs, half:] = (acc[3, rs, half:] + half_in[1, rs].astype(F32)).astype(BF16)
        sendb[3, rs, :half] = acc[3, rs, :half].astype(BF16)
        link.start(gl[dz], sendb.at[3, r], full_in.at[1, r], xl)

    def total(dz):
        r = pl.ds(dz * rows, rows)
        link.arrived(gr[dz], full_in.at[0, r], xl)
        link.arrived(gl[dz], full_in.at[1, r], xr)
        return acc[0, r] + full_in[0, r].astype(F32) + full_in[1, r].astype(F32)

    tables()
    fetch(0)
    around(0, 0)
    around(0, 1)
    fetch(1)
    fetch(2)
    pair(0)
    pair(1)
    fetch(3)
    fetch(4)
    fetch(5)
    own_weights()
    spread(0)
    forward(0, 0)
    forward(0, 1)
    spread(1)
    relay(0)
    tables_here()
    spread(2)
    last(0)
    relay(1)
    around(1, 0)
    own_weights_here()
    around(1, 1)
    first_half(0)
    last(1)
    spread(3)
    forward(1, 0)
    relay(2)
    spread(4)
    spread(5)
    forward(1, 1)
    relay(3)
    near(1)
    first_half(1)
    last(2)
    relay(4)
    near(3)
    first_half(3)
    relay(5)
    last(3)
    far()
    first_half(2)
    for a in range(3):
        shared(a)
    last(4)
    last(5)
    for dx in (2, 1):
        ffn(dx, 2, hid.at[dx])
    for a in range(3, 6):
        shared(a)
    send_far()
    ffn(3, 2, hid.at[3])
    acc[1] = second_half(1)
    acc[3] = second_half(3)
    send_near(1)
    ffn(0, 2, hid.at[0])
    acc[0] = second_half(0)
    send_near(0)
    taken = flag_ref[ex] == 1
    sg_ref[...] = jnp.where(taken, wgu[2, :, :ff], wgu[0, :, :ff])
    su_ref[...] = jnp.where(taken, wgu[2, :, ff:], wgu[0, :, ff:])
    sd_ref[...] = jnp.where(taken, wdn[2], wdn[0])
    sendb[0, rows:, :] = total(1).astype(BF16)
    fz = link.new()
    link.start(fz, sendb.at[0, pl.ds(rows, rows)], z_in, zp)
    t = total(0)
    link.arrived(fz, z_in, zp)
    mixed_ref[...] = (t + z_in[...].astype(F32)).astype(BF16)
    link.finish()


def finish(a, b, c, d, a_out, b_out, c_out, d_out, sem):
    pairs = ((a, a_out), (b, b_out), (c, c_out), (d, d_out))
    copies = [pltpu.make_async_copy(src, dst, sem.at[i]) for i, (src, dst) in enumerate(pairs)]
    for cp in copies:
        cp.start()
    for cp in copies:
        cp.wait()


def per_device(tokens, expert_ids, gate_probs, w_gate, w_up, w_down, placement, swap_flags):
    rows, width = tokens.shape
    ff = w_gate.shape[2]
    vmem = pl.BlockSpec(memory_space=pltpu.VMEM)
    smem = pl.BlockSpec(memory_space=pltpu.SMEM)
    hbm = pl.BlockSpec(memory_space=pltpu.HBM)
    shapes = (
        jax.ShapeDtypeStruct((rows, width), BF16),
        jax.ShapeDtypeStruct((width, ff), BF16),
        jax.ShapeDtypeStruct((width, ff), BF16),
        jax.ShapeDtypeStruct((ff, width), BF16),
    )
    blocks = (tokens, w_gate[0], w_up[0], w_down[0])
    blocks = tuple(pltpu.with_memory_space_constraint(b, pltpu.HBM) for b in blocks)
    results = pl.pallas_call(
        kernel,
        out_shape=shapes,
        in_specs=[vmem, vmem, smem, smem, hbm, hbm, hbm, hbm],
        out_specs=(vmem,) * 4,
        scratch_shapes=[
            pltpu.VMEM((4, 2 * rows, width), BF16),
            pltpu.VMEM((2, expert_ids.shape[1], 128), F32),
            pltpu.VMEM((8, 8, 128), F32),
            pltpu.VMEM((8, 8, 128), F32),
            pltpu.VMEM((4, 2 * rows, 8), F32),
            pltpu.VMEM((4, width, 2 * ff), BF16),
            pltpu.VMEM((4, ff, width), BF16),
            pltpu.VMEM((4, 2 * rows, 2 * ff), BF16),
            pltpu.VMEM((4, 2 * rows, width), F32),
            pltpu.VMEM((4, 2 * rows, width), BF16),
            pltpu.VMEM((2, 2 * rows, width // 2), BF16),
            pltpu.VMEM((2, 2 * rows, width), BF16),
            pltpu.VMEM((rows, width), BF16),
            pltpu.SemaphoreType.DMA((112,)),
            pltpu.SemaphoreType.DMA((112,)),
            pltpu.SemaphoreType.DMA((6,)),
        ],
        compiler_params=pltpu.CompilerParams(
            collective_id=0, has_side_effects=True, vmem_limit_bytes=48 * 2**20
        ),
    )(expert_ids.T, gate_probs.T, swap_flags, placement, *blocks)
    mixed, sg, su, sd = pl.pallas_call(
        finish,
        out_shape=shapes,
        in_specs=[pl.BlockSpec(memory_space=pl.ANY)] * 4,
        out_specs=[hbm] * 4,
        scratch_shapes=[pltpu.SemaphoreType.DMA((4,))],
        compiler_params=pltpu.CompilerParams(vmem_limit_bytes=2**20),
    )(*results)
    return mixed, sg[None], su[None], sd[None]


def solution(mesh):
    in_specs = (
        P(("dp", "expert"), None),
        P(("dp", "expert"), None),
        P(("dp", "expert"), None),
        P("expert", None, None),
        P("expert", None, None),
        P("expert", None, None),
        P(),
        P(),
    )
    out_specs = (
        P(("dp", "expert"), None),
        P(("dp", "expert"), None, None),
        P(("dp", "expert"), None, None),
        P(("dp", "expert"), None, None),
    )
    return jax.shard_map(
        per_device, mesh=mesh, in_specs=in_specs, out_specs=out_specs, check_vma=False
    )
```

time: 88.2 us -> 70.9 us (0.80)
  local copies, waits for them, and re-layouts: 9.91 us -> 0.68 us
  Pallas kernels: 77.1 us -> 68.4 us
    pallas_call x1 -> x2, Pallas kernels: 77.1 us -> 68.4 us  [the longest x1 66.9 us: per_device(): pl.pallas_call(kernel, out_shape=shapes, in_specs=[vmem, vmem, smem, smem...]
    unnamed x20 -> x8, local copies, waits for them, and re-layouts: 7.48 us -> 0.68 us
    broadcast_in_dim x6 -> x0, local copies, waits for them, and re-layouts: 0.98 us -> none  [the longest x1 0.65 us: per_device(): flag = jnp.broadcast_to(swap_flags[ex], (8, 128))]
where the time goes in v2:
time: 70.9 us; the launch traced here: 69.8 us
  Pallas kernels  68.4 us (96%)
    pallas_call x1, Pallas kernels, per_device(): pl.pallas_call(kernel, out_shape=shapes, in_specs=[vmem, vmem, smem, smem...  66.9 us
    pallas_call x1, Pallas kernels, per_device(): pl.pallas_call(finish, out_shape=shapes, in_specs=[pl.BlockSpec(memory_sp...  1.51 us

profile of v2, /device:TPU:1, one launch (start us, length us, event | category | flops | bytes accessed | tf_op | source)
XLA Modules:
  0.0 69.8 jit_solution(16400390113815983991)
XLA Ops:
  0.6 0.0 copy-start.1
  0.6 0.0 copy-start
  0.7 0.0 copy-start.2
  0.7 0.0 copy-start.3
  0.7 0.6 copy-done.1
  1.3 0.0 copy-done
  1.3 0.0 copy-done.2
  1.3 0.0 copy-done.3
  1.3 66.9 %shard_map.111 = (bf16[112,1024]{1,0:T(8,128)(2,1)S(1)}, bf16[1024,384]{1,0:T(8,128)(2,1)S(1)}, bf16[1024,384]{1,0:T(8,128)(2,1)S(1)}, bf16[384,1024]{1,0:T(8,128)(2,1)S(1)}) custom-call(s32[8,112]{1,0:T(8,128)S(1)} %bitcast.8, f32[8,112]{1,0:T(8,128)S(1)} %bitcast.9, s32[32]{0:T(128)S(1)} %copy-done.2, s32[32]{0:T(128)S(1)} %copy-done.3, ...), custom_call_target="tpu_custom_call" | custom-call | tf_op jit(solution)/shard_map/pallas_call | solution.py:403
  68.3 1.5 %shard_map.112 = (bf16[112,1024]{1,0:T(8,128)(2,1)}, bf16[1024,384]{1,0:T(8,128)(2,1)}, bf16[1024,384]{1,0:T(8,128)(2,1)}, bf16[384,1024]{1,0:T(8,128)(2,1)}) custom-call(bf16[112,1024]{1,0:T(8,128)(2,1)S(1)} %get-tuple-element.12.a, bf16[1024,384]{1,0:T(8,128)(2,1)S(1)} %get-tuple-element.13.b, bf16[1024,384]{1,0:T(8,128)(2,1)S(1)} %get-tuple-element.14.c, ...), custom_call_target="tpu_custom_call" | custom-call | tf_op jit(solution)/shard_map/pallas_call | solution.py:430
Async XLA Ops:
  0.6 0.7 copy-start.1
  0.6 0.7 copy-start
  0.7 0.7 copy-start.2
  0.7 0.7 copy-start.3

commit v3 on v2

--- a/solution.py
+++ b/solution.py
@@ -103,7 +103,7 @@
 
     link = Links(send_sem, recv_sem)
 
-    pieces = [(0, 0, 128), (0, 128, ff - 128), (1, 0, ff), (2, 0, half), (2, half, half // 2), (2, half + half // 2, half // 2)]
+    pieces = [(0, 0, 128), (0, 128, ff - 128), (1, 0, ff), (2, 0, half), (2, half, half)]
 
     def row_range(i, qi, h):
         n = (wd_hbm.shape[0] if i == 2 else width) // 4
@@ -124,7 +124,7 @@
         return (wg_hbm, wu_hbm, wd_hbm)[i].at[row_range(i, qi, h), pl.ds(c0, cn)]
 
     yp, ym, yo = (y + 1) % 4, (y + 3) % 4, (y + 2) % 4
-    direct = -1
+    direct = (3, 4)
 
     zk, ok = {}, {}
 
@@ -233,11 +233,11 @@
 
     def relay(a):
         link.arrived(yk[a, 0, 1], part(a, 2, ym, 0), down)
-        if a != direct:
+        if a not in direct:
             fk[a, 0] = link.new()
             link.start(fk[a, 0], part(a, 2, ym, 0), part(a, 2, ym, 0), up)
         link.arrived(yk[a, 1, -1], part(a, 2, yp, 1), up)
-        if a != direct:
+        if a not in direct:
             fk[a, 1] = link.new()
             link.start(fk[a, 1], part(a, 2, yp, 1), part(a, 2, yp, 1), down)
         link.arrived(yk[a, 1, 1], part(a, 2, ym, 1), down)
@@ -246,7 +246,7 @@
         share(a, yp)
 
     def last(a):
-        if a == direct:
+        if a in direct:
             link.arrived(ok[a, 0], part(a, 2, yo, 0), at_z(-2))
             link.arrived(ok[a, 1], part(a, 2, yo, 1), at_z(2))
         else:
@@ -272,38 +272,56 @@
         w = wdn[0:2].reshape(2 * ff, width)
         acc[dx] = jnp.dot(hid[dx], w, preferred_element_type=F32)
 
-    def second_half(dx):
-        w = wdn[2:4].reshape(2 * ff, width)
-        return acc[dx] + jnp.dot(hid[dx], w, preferred_element_type=F32)
-
-    hr, hl, gr, gl = {}, {}, {}, {}
-    low, high = pl.ds(0, half), pl.ds(half, half)
-
-    def send_far():
-        sendb[2] = second_half(2).astype(BF16)
-        for dz in (1, 0):
-            r = pl.ds(dz * rows, rows)
-            hr[dz], hl[dz] = link.new(), link.new()
-            link.start(hr[dz], sendb.at[2, r, low], half_in.at[0, r], xr)
-            link.start(hl[dz], sendb.at[2, r, high], half_in.at[1, r], xl)
-
-    def send_near(dz):
+    def second_half(dx, cc):
+        cols = pl.ds(cc * half, half)
+        w = wdn[2:4, :, cols].reshape(2 * ff, half)
+        return acc[dx, :, cols] + jnp.dot(hid[dx], w, preferred_element_type=F32)
+
+    quarter = half // 2
+    hr, hl, gr, gl, fz = {}, {}, {}, {}, {}
+
+    def send_far(cc):
+        c0 = cc * half
+        sendb[2, :, c0 : c0 + half] = second_half(2, cc).astype(BF16)
+        hr[cc], hl[cc] = link.new(), link.new()
+        link.start(hr[cc], sendb.at[2, :, pl.ds(c0, quarter)], half_in.at[0, cc], xr)
+        link.start(hl[cc], sendb.at[2, :, pl.ds(c0 + quarter, quarter)], half_in.at[1, cc], xl)
+
+    def own_sum(dx, cc):
+        acc[dx, :, cc * half : (cc + 1) * half] = second_half(dx, cc)
+
+    def send_near(cc, dz):
+        c0, c1, c2 = cc * half, cc * half + quarter, (cc + 1) * half
+        cols = pl.ds(c0, half)
+        if dz == 1:
+            link.arrived(hr[cc], half_in.at[0, cc], xl)
+            link.arrived(hl[cc], half_in.at[1, cc], xr)
         r, rs = pl.ds(dz * rows, rows), slice(dz * rows, (dz + 1) * rows)
-        gr[dz], gl[dz] = link.new(), link.new()
-        link.arrived(hr[dz], half_in.at[0, r], xl)
-        sendb[1, rs, :half] = (acc[1, rs, :half] + half_in[0, rs].astype(F32)).astype(BF16)
-        sendb[1, rs, half:] = acc[1, rs, half:].astype(BF16)
-        link.start(gr[dz], sendb.at[1, r], full_in.at[0, r], xr)
-        link.arrived(hl[dz], half_in.at[1, r], xr)
-        sendb[3, rs, half:] = (acc[3, rs, half:] + half_in[1, rs].astype(F32)).astype(BF16)
-        sendb[3, rs, :half] = acc[3, rs, :half].astype(BF16)
-        link.start(gl[dz], sendb.at[3, r], full_in.at[1, r], xl)
-
-    def total(dz):
-        r = pl.ds(dz * rows, rows)
-        link.arrived(gr[dz], full_in.at[0, r], xl)
-        link.arrived(gl[dz], full_in.at[1, r], xr)
-        return acc[0, r] + full_in[0, r].astype(F32) + full_in[1, r].astype(F32)
+        gr[cc, dz], gl[cc, dz] = link.new(), link.new()
+        sendb[1, rs, c0:c1] = (acc[1, rs, c0:c1] + half_in[0, cc, rs].astype(F32)).astype(BF16)
+        sendb[1, rs, c1:c2] = acc[1, rs, c1:c2].astype(BF16)
+        link.start(gr[cc, dz], sendb.at[1, r, cols], full_in.at[0, r, cols], xr)
+        sendb[3, rs, c0:c1] = acc[3, rs, c0:c1].astype(BF16)
+        sendb[3, rs, c1:c2] = (acc[3, rs, c1:c2] + half_in[1, cc, rs].astype(F32)).astype(BF16)
+        link.start(gl[cc, dz], sendb.at[3, r, cols], full_in.at[1, r, cols], xl)
+
+    def total(cc, dz):
+        cols, r = pl.ds(cc * half, half), pl.ds(dz * rows, rows)
+        link.arrived(gr[cc, dz], full_in.at[0, r, cols], xl)
+        link.arrived(gl[cc, dz], full_in.at[1, r, cols], xr)
+        return acc[0, r, cols] + full_in[0, r, cols].astype(F32) + full_in[1, r, cols].astype(F32)
+
+    def send_pair(cc):
+        cols, r = pl.ds(cc * half, half), pl.ds(rows, rows)
+        sendb[0, rows:, cc * half : (cc + 1) * half] = total(cc, 1).astype(BF16)
+        fz[cc] = link.new()
+        link.start(fz[cc], sendb.at[0, r, cols], z_in.at[:, cols], zp)
+
+    def final(cc):
+        cols = pl.ds(cc * half, half)
+        t = total(cc, 0)
+        link.arrived(fz[cc], z_in.at[:, cols], zp)
+        mixed_ref[:, cc * half : (cc + 1) * half] = (t + z_in[:, cols].astype(F32)).astype(BF16)
 
     tables()
     fetch(0)
@@ -314,8 +332,9 @@
     pair(0)
     pair(1)
     fetch(3)
+    fetch_opposite(3)
     fetch(4)
-    fetch(5)
+    fetch_opposite(4)
     own_weights()
     spread(0)
     forward(0, 0)
@@ -331,49 +350,50 @@
     around(1, 1)
     first_half(0)
     last(1)
+    forward(1, 0)
     spread(3)
-    forward(1, 0)
     relay(2)
     spread(4)
-    spread(5)
     forward(1, 1)
-    relay(3)
+    last(3)
     near(1)
     first_half(1)
     last(2)
-    relay(4)
     near(3)
     first_half(3)
-    relay(5)
-    last(3)
+    relay(3)
+    last(4)
     far()
     first_half(2)
     for a in range(3):
         shared(a)
-    last(4)
-    last(5)
-    for dx in (2, 1):
-        ffn(dx, 2, hid.at[dx])
-    for a in range(3, 6):
-        shared(a)
-    send_far()
+    ffn(2, 2, hid.at[2])
+    shared(3)
+    send_far(0)
+    relay(4)
+    ffn(1, 2, hid.at[1])
     ffn(3, 2, hid.at[3])
-    acc[1] = second_half(1)
-    acc[3] = second_half(3)
-    send_near(1)
+    shared(4)
+    send_far(1)
+    own_sum(1, 0)
+    own_sum(3, 0)
+    send_near(0, 1)
+    own_sum(1, 1)
+    own_sum(3, 1)
+    send_near(1, 1)
+    send_near(0, 0)
+    send_near(1, 0)
     ffn(0, 2, hid.at[0])
-    acc[0] = second_half(0)
-    send_near(0)
+    own_sum(0, 0)
+    own_sum(0, 1)
+    send_pair(0)
+    send_pair(1)
     taken = flag_ref[ex] == 1
     sg_ref[...] = jnp.where(taken, wgu[2, :, :ff], wgu[0, :, :ff])
     su_ref[...] = jnp.where(taken, wgu[2, :, ff:], wgu[0, :, ff:])
     sd_ref[...] = jnp.where(taken, wdn[2], wdn[0])
-    sendb[0, rows:, :] = total(1).astype(BF16)
-    fz = link.new()
-    link.start(fz, sendb.at[0, pl.ds(rows, rows)], z_in, zp)
-    t = total(0)
-    link.arrived(fz, z_in, zp)
-    mixed_ref[...] = (t + z_in[...].astype(F32)).astype(BF16)
+    final(0)
+    final(1)
     link.finish()
 
 
@@ -416,11 +436,11 @@
             pltpu.VMEM((4, 2 * rows, 2 * ff), BF16),
             pltpu.VMEM((4, 2 * rows, width), F32),
             pltpu.VMEM((4, 2 * rows, width), BF16),
-            pltpu.VMEM((2, 2 * rows, width // 2), BF16),
+            pltpu.VMEM((2, 2, 2 * rows, width // 4), BF16),
             pltpu.VMEM((2, 2 * rows, width), BF16),
             pltpu.VMEM((rows, width), BF16),
-            pltpu.SemaphoreType.DMA((112,)),
-            pltpu.SemaphoreType.DMA((112,)),
+            pltpu.SemaphoreType.DMA((128,)),
+            pltpu.SemaphoreType.DMA((128,)),
             pltpu.SemaphoreType.DMA((6,)),
         ],
         compiler_params=pltpu.CompilerParams(

time: 70.9 us -> 68 us (0.959)
  Pallas kernels: 68.4 us -> 65.8 us
    pallas_call x1, Pallas kernels: 66.9 us -> 64.3 us  [per_device(): pl.pallas_call(kernel, out_shape=shapes, in_specs=[vmem, vmem, smem, smem...]
where the time goes in v3:
time: 68 us; the launch traced here: 67.2 us
  Pallas kernels  65.8 us (97%)
  local copies, waits for them, and re-layouts  0.68 us (1%)
  between operations  0.68 us (1%)
    pallas_call x1, Pallas kernels, per_device(): pl.pallas_call(kernel, out_shape=shapes, in_specs=[vmem, vmem, smem, smem...  64.3 us
    pallas_call x1, Pallas kernels, per_device(): pl.pallas_call(finish, out_shape=shapes, in_specs=[pl.BlockSpec(memory_sp...  1.51 us

profile of v3, /device:TPU:1, one launch (start us, length us, event | category | flops | bytes accessed | tf_op | source)
XLA Modules:
  0.0 67.2 jit_solution(2069797305810206523)
XLA Ops:
  0.6 0.0 copy-start.1
  0.6 0.0 copy-start
  0.7 0.0 copy-start.2
  0.7 0.0 copy-start.3
  0.7 0.6 copy-done.1
  1.3 0.0 copy-done
  1.3 0.0 copy-done.2
  1.3 0.0 copy-done.3
  1.3 64.3 %shard_map.111 = (bf16[112,1024]{1,0:T(8,128)(2,1)S(1)}, bf16[1024,384]{1,0:T(8,128)(2,1)S(1)}, bf16[1024,384]{1,0:T(8,128)(2,1)S(1)}, bf16[384,1024]{1,0:T(8,128)(2,1)S(1)}) custom-call(s32[8,112]{1,0:T(8,128)S(1)} %bitcast.8, f32[8,112]{1,0:T(8,128)S(1)} %bitcast.9, s32[32]{0:T(128)S(1)} %copy-done.2, s32[32]{0:T(128)S(1)} %copy-done.3, ...), custom_call_target="tpu_custom_call" | custom-call | tf_op jit(solution)/shard_map/pallas_call | solution.py:423
  65.7 1.5 %shard_map.112 = (bf16[112,1024]{1,0:T(8,128)(2,1)}, bf16[1024,384]{1,0:T(8,128)(2,1)}, bf16[1024,384]{1,0:T(8,128)(2,1)}, bf16[384,1024]{1,0:T(8,128)(2,1)}) custom-call(bf16[112,1024]{1,0:T(8,128)(2,1)S(1)} %get-tuple-element.12.a, bf16[1024,384]{1,0:T(8,128)(2,1)S(1)} %get-tuple-element.13.b, bf16[1024,384]{1,0:T(8,128)(2,1)S(1)} %get-tuple-element.14.c, ...), custom_call_target="tpu_custom_call" | custom-call | tf_op jit(solution)/shard_map/pallas_call | solution.py:450
Async XLA Ops:
  0.6 0.7 %copy-start.1 = (f32[112,8]{0,1:T(8,128)S(1)}, f32[112,8]{0,1:T(8,128)}, u32[]{:S(2)}) copy-start(f32[112,8]{0,1:T(8,128)} %param.10) | copy-start | bytes 10756
  0.6 0.7 %copy-start = (s32[112,8]{0,1:T(8,128)S(1)}, s32[112,8]{0,1:T(8,128)}, u32[]{:S(2)}) copy-start(s32[112,8]{0,1:T(8,128)} %param.9) | copy-start | bytes 10756
  0.7 0.7 %copy-start.2 = (s32[32]{0:T(128)S(1)}, s32[32]{0:T(128)}, u32[]{:S(2)}) copy-start(s32[32]{0:T(128)} %flag_ref.1) | copy-start | bytes 388
  0.7 0.7 %copy-start.3 = (s32[32]{0:T(128)S(1)}, s32[32]{0:T(128)}, u32[]{:S(2)}) copy-start(s32[32]{0:T(128)} %place_ref.1) | copy-start | bytes 388

commit v4 on v3

--- a/solution.py
+++ b/solution.py
@@ -42,9 +42,9 @@
 
 
 def kernel(
-    ids_ref, prob_ref, flag_ref, place_ref, tok_hbm, wg_hbm, wu_hbm, wd_hbm,
+    ids_hbm, prob_hbm, flag_ref, place_ref, tok_hbm, wg_hbm, wu_hbm, wd_hbm,
     mixed_ref, sg_ref, su_ref, sd_ref,
-    x_buf, flip, table_ref, meta, gcol, wgu, wdn, hid, acc, sendb, half_in, full_in, z_in,
+    x_buf, ids_buf, prob_buf, flip, table_ref, meta, gcol, wgu, wdn, hid, acc, sendb, half_in, full_in, z_in,
     send_sem, recv_sem, local_sem,
 ):
     rows, width = tok_hbm.shape
@@ -71,6 +71,12 @@
     peers = [at(1, False), at(-1, False), at(2, False), at(0, True), at(1, True), at(-1, True), at(2, True)]
     partners = peers + [at_z(2), at_z(-2), at_y(1), at_y(-1), sibling]
 
+    routes = [
+        pltpu.make_async_copy(ids_hbm, ids_buf, local_sem.at[4]),
+        pltpu.make_async_copy(prob_hbm, prob_buf, local_sem.at[5]),
+    ]
+    for cp in routes:
+        cp.start()
     barrier = pltpu.get_barrier_semaphore()
     for dev in partners:
         pl.semaphore_signal(barrier, inc=1, device_id=dev, device_id_type=MESH)
@@ -86,8 +92,10 @@
         cp.start()
 
     flip[...] = jnp.zeros_like(flip)
-    flip[0, :, 0:rows] = ids_ref[...].astype(F32)
-    flip[1, :, 0:rows] = prob_ref[...]
+    for cp in routes:
+        cp.wait()
+    flip[0, :, 0:rows] = ids_buf[...].astype(F32)
+    flip[1, :, 0:rows] = prob_buf[...]
     ids_t, prob_t = flip[0], flip[1]
     for dx in range(4):
         for dz in range(2):
@@ -332,8 +340,8 @@
     pair(0)
     pair(1)
     fetch(3)
+    fetch(4)
     fetch_opposite(3)
-    fetch(4)
     fetch_opposite(4)
     own_weights()
     spread(0)
@@ -418,15 +426,17 @@
         jax.ShapeDtypeStruct((width, ff), BF16),
         jax.ShapeDtypeStruct((ff, width), BF16),
     )
-    blocks = (tokens, w_gate[0], w_up[0], w_down[0])
-    blocks = tuple(pltpu.with_memory_space_constraint(b, pltpu.HBM) for b in blocks)
+    blocks = (expert_ids.T, gate_probs.T, swap_flags, placement, tokens, w_gate[0], w_up[0], w_down[0])
+    ids, probs, flags, places, *blocks = (pltpu.with_memory_space_constraint(b, pltpu.HBM) for b in blocks)
     results = pl.pallas_call(
         kernel,
         out_shape=shapes,
-        in_specs=[vmem, vmem, smem, smem, hbm, hbm, hbm, hbm],
+        in_specs=[hbm, hbm, smem, smem, hbm, hbm, hbm, hbm],
         out_specs=(vmem,) * 4,
         scratch_shapes=[
             pltpu.VMEM((4, 2 * rows, width), BF16),
+            pltpu.VMEM(expert_ids.shape[::-1], jnp.int32),
+            pltpu.VMEM(expert_ids.shape[::-1], F32),
             pltpu.VMEM((2, expert_ids.shape[1], 128), F32),
             pltpu.VMEM((8, 8, 128), F32),
             pltpu.VMEM((8, 8, 128), F32),
@@ -446,7 +456,7 @@
         compiler_params=pltpu.CompilerParams(
             collective_id=0, has_side_effects=True, vmem_limit_bytes=48 * 2**20
         ),
-    )(expert_ids.T, gate_probs.T, swap_flags, placement, *blocks)
+    )(ids, probs, flags, places, *blocks)
     mixed, sg, su, sd = pl.pallas_call(
         finish,
         out_shape=shapes,

time: 68 us -> 67.3 us (0.990)
  local copies, waits for them, and re-layouts: 0.68 us -> 0 us
where the time goes in v4:
time: 67.3 us; the launch traced here: 66.5 us
  Pallas kernels  65.8 us (98%)
    pallas_call x1, Pallas kernels, per_device(): pl.pallas_call(kernel, out_shape=shapes, in_specs=[hbm, hbm, smem, smem,...  64.3 us
    pallas_call x1, Pallas kernels, per_device(): pl.pallas_call(finish, out_shape=shapes, in_specs=[pl.BlockSpec(memory_sp...  1.51 us

profile of v4, /device:TPU:1, one launch (start us, length us, event | category | flops | bytes accessed | tf_op | source)
XLA Modules:
  0.0 66.5 jit_solution(5452700340261461055)
XLA Ops:
  0.6 64.3 %shard_map.111 = (bf16[112,1024]{1,0:T(8,128)(2,1)S(1)}, bf16[1024,384]{1,0:T(8,128)(2,1)S(1)}, bf16[1024,384]{1,0:T(8,128)(2,1)S(1)}, bf16[384,1024]{1,0:T(8,128)(2,1)S(1)}) custom-call(s32[8,112]{1,0:T(8,128)} %bitcast.11, f32[8,112]{1,0:T(8,128)} %bitcast.12, s32[32]{0:T(128)} %flag_ref.1, s32[32]{0:T(128)} %place_ref.1, bf16[112,1024]{1,0:T(8,128)(2,1)} %tok_hbm.1, ...), custom_call_target="tpu_custom_call" | custom-call | tf_op jit(solution)/shard_map/pallas_call | solution.py:431
  65.0 1.5 %shard_map.112 = (bf16[112,1024]{1,0:T(8,128)(2,1)}, bf16[1024,384]{1,0:T(8,128)(2,1)}, bf16[1024,384]{1,0:T(8,128)(2,1)}, bf16[384,1024]{1,0:T(8,128)(2,1)}) custom-call(bf16[112,1024]{1,0:T(8,128)(2,1)S(1)} %get-tuple-element.12.a, bf16[1024,384]{1,0:T(8,128)(2,1)S(1)} %get-tuple-element.13.b, bf16[1024,384]{1,0:T(8,128)(2,1)S(1)} %get-tuple-element.14.c, ...), custom_call_target="tpu_custom_call" | custom-call | tf_op jit(solution)/shard_map/pallas_call | solution.py:460

commit v5 on v4

--- a/solution.py
+++ b/solution.py
@@ -368,7 +368,6 @@
     first_half(1)
     last(2)
     near(3)
-    first_half(3)
     relay(3)
     last(4)
     far()
@@ -380,6 +379,7 @@
     send_far(0)
     relay(4)
     ffn(1, 2, hid.at[1])
+    first_half(3)
     ffn(3, 2, hid.at[3])
     shared(4)
     send_far(1)

time: 67.3 us -> 67.5 us (level)
  Pallas kernels: 65.8 us -> 66.7 us
    pallas_call x1, Pallas kernels: 64.3 us -> 65.2 us  [per_device(): pl.pallas_call(kernel, out_shape=shapes, in_specs=[hbm, hbm, smem, smem,...]
where the time goes in v5:
time: 67.5 us; the launch traced here: 67.4 us
  Pallas kernels  66.7 us (99%)
    pallas_call x1, Pallas kernels, per_device(): pl.pallas_call(kernel, out_shape=shapes, in_specs=[hbm, hbm, smem, smem,...  65.2 us
    pallas_call x1, Pallas kernels, per_device(): pl.pallas_call(finish, out_shape=shapes, in_specs=[pl.BlockSpec(memory_sp...  1.51 us

profile of v5, /device:TPU:1, one launch (start us, length us, event | category | flops | bytes accessed | tf_op | source)
XLA Modules:
  0.0 67.4 jit_solution(12262659168588953662)
XLA Ops:
  0.6 65.2 %shard_map.111 = (bf16[112,1024]{1,0:T(8,128)(2,1)S(1)}, bf16[1024,384]{1,0:T(8,128)(2,1)S(1)}, bf16[1024,384]{1,0:T(8,128)(2,1)S(1)}, bf16[384,1024]{1,0:T(8,128)(2,1)S(1)}) custom-call(s32[8,112]{1,0:T(8,128)} %bitcast.11, f32[8,112]{1,0:T(8,128)} %bitcast.12, s32[32]{0:T(128)} %flag_ref.1, s32[32]{0:T(128)} %place_ref.1, bf16[112,1024]{1,0:T(8,128)(2,1)} %tok_hbm.1, ...), custom_call_target="tpu_custom_call" | custom-call | tf_op jit(solution)/shard_map/pallas_call | solution.py:431
  65.8 1.5 %shard_map.112 = (bf16[112,1024]{1,0:T(8,128)(2,1)}, bf16[1024,384]{1,0:T(8,128)(2,1)}, bf16[1024,384]{1,0:T(8,128)(2,1)}, bf16[384,1024]{1,0:T(8,128)(2,1)}) custom-call(bf16[112,1024]{1,0:T(8,128)(2,1)S(1)} %get-tuple-element.12.a, bf16[1024,384]{1,0:T(8,128)(2,1)S(1)} %get-tuple-element.13.b, bf16[1024,384]{1,0:T(8,128)(2,1)S(1)} %get-tuple-element.14.c, ...), custom_call_target="tpu_custom_call" | custom-call | tf_op jit(solution)/shard_map/pallas_call | solution.py:460
